TPU v7x, 32 devices: a whole 2x2x4 slice. The times are simulated.
32 devices in a mesh: orb: 4 (over z), tile: 8 (over y, x, core).
Axes of the slice: x: 2, y: 2, z: 4, core: 2. Of those that a mesh axis runs over, the one named last changes fastest.
Arguments:
- basis_values: bfloat16 [2048, 65536], P('tile'), may hold values from -6 to 6
- coefficients: bfloat16 [65536, 128], P('tile', 'orb'), may hold values from -0.03125 to 0.03125
- occupations: float32 [128], P('orb'), may hold values from 0.5 to 2
- owners: int32 [2048, 1], P('tile'), may hold values from 0 to 7; in each aligned block of 256 rows (0 to 255, 256 to 511, ...) at most 64 rows name the same one
- offsets: int32 [2048], P('tile'), may hold values from 0 to 8191
Outputs:
- density: float32 [64, 64, 128], P('tile', 'orb')
- gradient: float32 [3, 64, 64, 128], P(None, 'tile', 'orb')
Inputs may be any that keep to these rules, and one draw needn't show every extreme that they name: `owners`: at most 64 entries of one tile's list name the same owner, and some tile's list reaches 64.
All inputs are finite; a program needn't handle non-finite values.
Results may differ from a plain program's by a relative error of at most 0.0003.
Values may be sent and summed in bfloat16 or wider, within the bound.
A program may use at most 320 MiB of HBM per device.

v0:
```python
import jax
import jax.numpy as jnp
from jax import lax
from jax.sharding import PartitionSpec as P

CY = 64
CZ = 128


def with_halo(cells, sides, width):
    for axis, dim in sides:
        count = lax.axis_size(axis)
        ends = count - 1
        head = lax.slice_in_dim(cells, 0, width, axis=dim)
        tail = lax.slice_in_dim(cells, cells.shape[dim] - width, cells.shape[dim], axis=dim)
        cells = jnp.concatenate(
            [
                lax.ppermute(tail, axis, [(i, (i + 1) % count) for i in range(ends)]),
                cells,
                lax.ppermute(head, axis, [((i + 1) % count, i) for i in range(ends)]),
            ],
            axis=dim,
        )
    return cells


def central(padded):
    along_x = 0.5 * (padded[2:, 1:-1, 1:-1] - padded[:-2, 1:-1, 1:-1])
    along_y = 0.5 * (padded[1:-1, 2:, 1:-1] - padded[1:-1, :-2, 1:-1])
    along_z = 0.5 * (padded[1:-1, 1:-1, 2:] - padded[1:-1, 1:-1, :-2])
    return jnp.stack([along_x, along_y, along_z])


def body(basis_values, coefficients, occupations, owners, offsets):
    listed_count = owners.shape[0]
    rows_held = coefficients.shape[0]
    local_orbitals = coefficients.shape[1]
    owner_ids = owners[:, 0]
    global_rows = owner_ids * rows_held + offsets
    empty = jnp.zeros((listed_count, local_orbitals), jnp.bfloat16)
    shard_rows = lax.all_gather(coefficients, "tile", axis=0, tiled=True)
    inside = (global_rows >= 0) & (global_rows < shard_rows.shape[0])
    safe_rows = jnp.clip(global_rows, 0, shard_rows.shape[0] - 1)
    taken = jnp.take(shard_rows, safe_rows, axis=0)
    listed = jnp.where(inside[:, None], taken, empty)
    depth_cells = basis_values.shape[1] // (CY * CZ)
    share_width = CY // lax.axis_size("orb")
    orbitals = jnp.einsum("bo,bc->oc", listed, basis_values, preferred_element_type=jnp.float32)
    partial_value = jnp.sum(occupations[:, None] * orbitals * orbitals, axis=0).reshape(
        depth_cells, CY, CZ
    )
    density_full = lax.psum(partial_value, "orb")
    padded = with_halo(density_full, (("tile", 0),), 1)
    padded = jnp.pad(padded, ((0, 0), (1, 1), (1, 1)))
    first_col = lax.axis_index("orb") * share_width
    density = lax.dynamic_slice_in_dim(density_full, first_col, share_width, 1)
    gradient = lax.dynamic_slice_in_dim(central(padded), first_col, share_width, 2)
    return (density, gradient)


def solution(mesh):
    placed = (P("tile", None), P("tile", "orb"), P("orb"), P("tile", None), P("tile"))
    return jax.shard_map(
        body,
        mesh=mesh,
        in_specs=placed,
        out_specs=(P("tile", "orb", None), P(None, "tile", "orb", None)),
        check_vma=False,
    )
```

profile of v0, /device:TPU:4, one launch (start us, length us, event | category | flops | bytes accessed | tf_op | source)
XLA Modules:
  0.0 181.8 jit_solution(3366293693858491619)
XLA Ops:
  7.2 0.0 all-gather.2.cloned.1.call-start
  7.2 2.7 %copy.7 = bf16[8192,32]{1,0:T(8,128)(2,1)} copy(bf16[8192,32]{0,1:T(8,128)(2,1)} %param.6) | data formatting | bytes 1048576 | tf_op args[1]
  9.9 0.0 all-gather.2.cloned.1.call-update
  9.9 0.0 all-reduce.3.cloned.1.call-start
  10.0 0.7 broadcast_multiply_fusion
  10.6 0.7 compare_and_fusion
  11.3 88.9 %all-gather.2.cloned.1.call-done = bf16[65536,32]{1,0:T(8,128)(2,1)} async-done(((bf16[8192,32]{1,0:T(8,128)(2,1)}), bf16[65536,32]{1,0:T(8,128)(2,1)}) %all-gather.2.cloned.1.call-update) | async-done | bytes 4194320 | tf_op jit(solution)/shard_map/all_gather | solution.py:41
  100.3 8.7 %gather_fusion = bf16[256,32]{1,0:T(8,128)(2,1)S(1)} fusion(bf16[65536,32]{1,0:T(8,128)(2,1)} %all-gather.2.cloned.1.call-done, s32[1024]{0:T(1024)S(1)} %pad_clamp_fusion), kind=kCustom, calls=%fused_computation | custom fusion | bytes 33792 | tf_op jit(solution)/shard_map/jit(_take)/gather | solution.py:44
  108.9 17.4 %fusion = f32[65536]{0:T(1024)} fusion(f32[32]{0:T(128)} %param.7, bf16[256,65536]{1,0:T(8,128)(2,1)} %param.5, bf16[256,32]{1,0:T(8,128)(2,1)S(1)} %gather_fusion, pred[256]{0:T(512)(128)(4,1)S(1)} %get-tuple-element.2, pred[256]{0:T(512)(128)(4,1)S(1)} %get-tuple-element.8), kind=kOutput, calls=%fused_computation.2 | convolution fusion | flops 1079984128 | bytes 33833600 | tf_op jit(solution)/shard_map/bo,bc->oc/dot_general | solution.py:48
  126.3 0.0 all-reduce.3.cloned.1.call-update
  126.4 36.5 %all-reduce.3.cloned.1.call-done = f32[8,64,128]{2,1,0:T(8,128)} async-done(((f32[8,64,128]{2,1,0:T(8,128)}), f32[8,64,128]{2,1,0:T(8,128)}) %all-reduce.3.cloned.1.call-update) | async-done | bytes 262160 | tf_op jit(solution)/shard_map/psum | solution.py:52
  162.8 0.8 fusion.24
  163.6 1.9 %collective-permute-start = (f32[1,64,128]{2,1,0:T(8,128)S(1)}, f32[1,64,128]{2,1,0:T(8,128)S(1)}, u32[]{:S(2)}, u32[]{:S(2)}) collective-permute-start(f32[1,64,128]{2,1,0:T(8,128)S(1)} %get-tuple-element.6), channel_id=1, source_target_pairs={{1,0},{2,1},{3,2},{4,3},{5,4},{6,5},{7,6},{9,8},{10,9},{11,10},{12... | collective-permute-start | bytes 98312 | tf_op jit(solution)/shard_map/ppermute | solution.py:20
  165.5 2.4 %collective-permute-start.1 = (f32[1,64,128]{2,1,0:T(8,128)S(1)}, f32[1,64,128]{2,1,0:T(8,128)S(1)}, u32[]{:S(2)}, u32[]{:S(2)}) collective-permute-start(f32[1,64,128]{2,1,0:T(8,128)S(1)} %get-tuple-element.7), channel_id=1, source_target_pairs={{0,1},{1,2},{2,3},{3,4},{4,5},{5,6},{6,7},{8,9},{9,10},{10,11},{11... | collective-permute-start | bytes 98312 | tf_op jit(solution)/shard_map/ppermute | solution.py:18
  167.9 1.5 constant_dynamic-slice_fusion
  169.4 0.0 collective-permute-done
  169.4 2.2 %collective-permute-done.1 = f32[1,64,128]{2,1,0:T(8,128)S(1)} collective-permute-done((f32[1,64,128]{2,1,0:T(8,128)S(1)}, f32[1,64,128]{2,1,0:T(8,128)S(1)}, u32[]{:S(2)}, u32[]{:S(2)}) %collective-permute-start.1) | collective-permute-done | bytes 32800 | tf_op jit(solution)/shard_map/ppermute | solution.py:18
  171.7 1.2 select_maximum_fusion
  172.9 1.3 fusion.5
  174.2 0.7 fusion.12
  (1 shorter events, 0.0 us)
Async XLA Ops:
  7.2 93.1 %all-gather.2.cloned.1.call-start = ((), (), s32[]{:S(2)}) async-start(), calls=%async_computation | async-start | bytes 18874368 | tf_op jit(solution)/shard_map/all_gather | solution.py:41
  9.9 152.9 %all-reduce.3.cloned.1.call-start = ((), (), s32[]{:S(2)}) async-start(), calls=%async_computation.1 | async-start | bytes 524288 | tf_op jit(solution)/shard_map/psum | solution.py:52
  163.6 5.8 %collective-permute-start = (f32[1,64,128]{2,1,0:T(8,128)S(1)}, f32[1,64,128]{2,1,0:T(8,128)S(1)}, u32[]{:S(2)}, u32[]{:S(2)}) collective-permute-start(f32[1,64,128]{2,1,0:T(8,128)S(1)} %get-tuple-element.6), channel_id=1, source_target_pairs={{1,0},{2,1},{3,2},{4,3},{5,4},{6,5},{7,6},{9,8},{10,9},{11,10},{12... | collective-permute-start | bytes 98312 | tf_op jit(solution)/shard_map/ppermute | solution.py:20
  165.5 6.1 %collective-permute-start.1 = (f32[1,64,128]{2,1,0:T(8,128)S(1)}, f32[1,64,128]{2,1,0:T(8,128)S(1)}, u32[]{:S(2)}, u32[]{:S(2)}) collective-permute-start(f32[1,64,128]{2,1,0:T(8,128)S(1)} %get-tuple-element.7), channel_id=1, source_target_pairs={{0,1},{1,2},{2,3},{3,4},{4,5},{5,6},{6,7},{8,9},{9,10},{10,11},{11... | collective-permute-start | bytes 98312 | tf_op jit(solution)/shard_map/ppermute | solution.py:18
Sparse Core Ops, SparseCore 0:
  10.0 90.1 all-gather.1
  126.5 36.3 all-reduce.2
where the time goes:
time: 182 us
  waiting for transfers between devices  128 us (70%)
  matrix products  17.4 us (10%)
  between operations  14.1 us (8%)
  local copies, waits for them, and re-layouts  13.6 us (7%)
  other arithmetic  4.62 us (3%)
  starting transfers between devices  4.39 us (2%)
    all_gather x1, waiting for transfers between devices, body(): shard_rows = lax.all_gather(coefficients, 'tile', axis=0, tiled=True)  88.9 us
    psum x1, waiting for transfers between devices, body(): density_full = lax.psum(partial_value, 'orb')  36.5 us
    dot_general x1, matrix products, body(): jnp.einsum('bo,bc->oc', listed, basis_values, preferred_element_type=jnp....  17.4 us
    gather x1, local copies, waits for them, and re-layouts, body(): taken = jnp.take(shard_rows, safe_rows, axis=0)  8.65 us
  transfers between devices with their start and end apart: 4, of which 3 were waited for; matrix products, arithmetic and copies ran while one was open for 2% of the time, Pallas kernels for 0%

commit v1 on v0

--- a/solution.py
+++ b/solution.py
@@ -38,7 +38,21 @@
     owner_ids = owners[:, 0]
     global_rows = owner_ids * rows_held + offsets
     empty = jnp.zeros((listed_count, local_orbitals), jnp.bfloat16)
-    shard_rows = lax.all_gather(coefficients, "tile", axis=0, tiled=True)
+    mine = coefficients
+    r_now = lax.axis_size("tile")
+    answer = lax.axis_index("tile")
+    u1, e_now, p_next = (r_now, answer, mine.shape[0])
+    line_up = [jj * u1 if num == 0 else jj for num, jj in enumerate(mine.shape)]
+    shard_rows = lax.dynamic_update_slice_in_dim(
+        jnp.zeros(line_up, mine.dtype), mine, e_now * p_next, axis=0
+    )
+    b = 1
+    while b < u1:
+        mine = lax.ppermute(mine, "tile", [(num, (num + 1) % u1) for num in range(u1)])
+        shard_rows = lax.dynamic_update_slice_in_dim(
+            shard_rows, mine, (e_now - b) % u1 * p_next, axis=0
+        )
+        b = b + 1
     inside = (global_rows >= 0) & (global_rows < shard_rows.shape[0])
     safe_rows = jnp.clip(global_rows, 0, shard_rows.shape[0] - 1)
     taken = jnp.take(shard_rows, safe_rows, axis=0)

time: 182 us -> 165 us (0.907)
  waiting for transfers between devices: 128 us -> 85 us
  local copies, waits for them, and re-layouts: 13.6 us -> 37.8 us
  starting transfers between devices: 4.39 us -> 6.47 us
    all_gather x1 -> x0, waiting for transfers between devices: 88.9 us -> none  [body(): shard_rows = lax.all_gather(coefficients, 'tile', axis=0, tiled=True)]
    ppermute x0 -> x7, waiting for transfers between devices: none -> 46.7 us  [body(): lax.ppermute(mine, 'tile', [(num, (num + 1) % u1) for num in range(u1)])]
    dynamic_update_slice x0 -> x8, local copies, waits for them, and re-layouts: none -> 11.7 us  [the longest x7 10.2 us: body(): lax.dynamic_update_slice_in_dim(shard_rows, mine, (e_now - b) % u1 * p_ne...]
    ppermute x0 -> x7, local copies, waits for them, and re-layouts: none -> 7.21 us  [body(): lax.ppermute(mine, 'tile', [(num, (num + 1) % u1) for num in range(u1)])]
    broadcast_in_dim x0 -> x1, local copies, waits for them, and re-layouts: none -> 6.02 us  [body(): jnp.zeros(line_up, mine.dtype)]
    ppermute x0 -> x7, starting transfers between devices: none -> 2.11 us  [body(): lax.ppermute(mine, 'tile', [(num, (num + 1) % u1) for num in range(u1)])]
  transfers between devices with their start and end apart: 4 -> 10, of which waited for: 3 -> 8; matrix products, arithmetic and copies ran while one was open for 2% -> 12% of each run, Pallas kernels for 0% -> 0%
where the time goes in v1:
time: 165 us; the launch traced here: 164 us
  waiting for transfers between devices  85 us (52%)
  local copies, waits for them, and re-layouts  37.8 us (23%)
  matrix products  17.4 us (11%)
  between operations  14.4 us (9%)
  starting transfers between devices  6.47 us (4%)
  other arithmetic  3.26 us (2%)
    ppermute x7, waiting for transfers between devices, body(): lax.ppermute(mine, 'tile', [(num, (num + 1) % u1) for num in range(u1)])  46.7 us
    psum x1, waiting for transfers between devices, body(): density_full = lax.psum(partial_value, 'orb')  36 us
    dot_general x1, matrix products, body(): jnp.einsum('bo,bc->oc', listed, basis_values, preferred_element_type=jnp....  17.4 us
    dynamic_update_slice x7, local copies, waits for them, and re-layouts, body(): lax.dynamic_update_slice_in_dim(shard_rows, mine, (e_now - b) % u1 * p_ne...  10.2 us
    gather x1, local copies, waits for them, and re-layouts, body(): taken = jnp.take(shard_rows, safe_rows, axis=0)  8.65 us
    ppermute x7, local copies, waits for them, and re-layouts, body(): lax.ppermute(mine, 'tile', [(num, (num + 1) % u1) for num in range(u1)])  7.21 us
    broadcast_in_dim x1, local copies, waits for them, and re-layouts, body(): jnp.zeros(line_up, mine.dtype)  6.02 us
  transfers between devices with their start and end apart: 10, of which 8 were waited for; matrix products, arithmetic and copies ran while one was open for 12% of the time, Pallas kernels for 0%

profile of v1, /device:TPU:4, one launch (start us, length us, event | category | flops | bytes accessed | tf_op | source)
XLA Modules:
  0.0 164.3 jit_solution(10770106793513225132)
XLA Ops:
  7.3 1.9 %copy.9 = bf16[8192,32]{1,0:T(8,128)(2,1)S(1)} copy(bf16[8192,32]{0,1:T(8,128)(2,1)} %param.6) | data formatting | bytes 1048576 | tf_op args[1]
  9.4 6.0 %broadcast_in_dim.30 = bf16[65536,32]{1,0:T(8,128)(2,1)} broadcast(bf16[]{:T(256)} %constant.84.clone.1), dimensions={} | broadcast | bytes 4194306 | tf_op jit(solution)/shard_map/broadcast_in_dim | solution.py:47
  15.4 1.5 constant_dynamic-update-slice_fusion.7
  17.0 1.0 copy.10
  18.0 1.6 collective-permute-start.1
  19.6 1.5 constant_dynamic-update-slice_fusion.6
  21.1 6.5 %collective-permute-done.1 = bf16[8192,32]{0,1:T(8,128)(2,1)S(1)} collective-permute-done((bf16[8192,32]{0,1:T(8,128)(2,1)S(1)}, bf16[8192,32]{0,1:T(8,128)(2,1)S(1)}, u32[]{:S(2)}, u32[]{:S(2)}) %collective-permute-start.1) | collective-permute-done | bytes 524320 | tf_op jit(solution)/shard_map/ppermute | solution.py:51
  27.6 1.0 copy.11
  28.7 1.5 constant_dynamic-update-slice_fusion.5
  30.2 8.0 %collective-permute-done.2 = bf16[8192,32]{0,1:T(8,128)(2,1)S(1)} collective-permute-done((bf16[8192,32]{0,1:T(8,128)(2,1)S(1)}, bf16[8192,32]{0,1:T(8,128)(2,1)S(1)}, u32[]{:S(2)}, u32[]{:S(2)}) %collective-permute-start.2) | collective-permute-done | bytes 524320 | tf_op jit(solution)/shard_map/ppermute | solution.py:51
  38.2 1.0 copy.12
  39.3 1.5 constant_dynamic-update-slice_fusion.4
  40.7 8.0 %collective-permute-done.3 = bf16[8192,32]{0,1:T(8,128)(2,1)S(1)} collective-permute-done((bf16[8192,32]{0,1:T(8,128)(2,1)S(1)}, bf16[8192,32]{0,1:T(8,128)(2,1)S(1)}, u32[]{:S(2)}, u32[]{:S(2)}) %collective-permute-start.3) | collective-permute-done | bytes 524320 | tf_op jit(solution)/shard_map/ppermute | solution.py:51
  48.8 1.0 copy.13
  49.9 1.5 constant_dynamic-update-slice_fusion.3
  51.4 8.0 %collective-permute-done.4 = bf16[8192,32]{0,1:T(8,128)(2,1)S(1)} collective-permute-done((bf16[8192,32]{0,1:T(8,128)(2,1)S(1)}, bf16[8192,32]{0,1:T(8,128)(2,1)S(1)}, u32[]{:S(2)}, u32[]{:S(2)}) %collective-permute-start.4) | collective-permute-done | bytes 524320 | tf_op jit(solution)/shard_map/ppermute | solution.py:51
  60.5 1.4 constant_dynamic-update-slice_fusion.2
  61.9 8.1 %collective-permute-done.5 = bf16[8192,32]{0,1:T(8,128)(2,1)S(1)} collective-permute-done((bf16[8192,32]{0,1:T(8,128)(2,1)S(1)}, bf16[8192,32]{0,1:T(8,128)(2,1)S(1)}, u32[]{:S(2)}, u32[]{:S(2)}) %collective-permute-start.5) | collective-permute-done | bytes 524320 | tf_op jit(solution)/shard_map/ppermute | solution.py:51
  70.0 1.0 copy.15
  71.3 1.5 constant_dynamic-update-slice_fusion.1
  72.7 8.0 %collective-permute-done.6 = bf16[8192,32]{0,1:T(8,128)(2,1)S(1)} collective-permute-done((bf16[8192,32]{0,1:T(8,128)(2,1)S(1)}, bf16[8192,32]{0,1:T(8,128)(2,1)S(1)}, u32[]{:S(2)}, u32[]{:S(2)}) %collective-permute-start.6) | collective-permute-done | bytes 524320 | tf_op jit(solution)/shard_map/ppermute | solution.py:51
  80.8 1.0 copy.16
  81.8 1.5 constant_dynamic-update-slice_fusion
  83.2 8.7 %gather_fusion = bf16[256,32]{1,0:T(8,128)(2,1)S(1)} fusion(bf16[65536,32]{1,0:T(8,128)(2,1)} %constant_dynamic-update-slice_fusion, s32[1024]{0:T(1024)S(1)} %pad_clamp_fusion), kind=kCustom, calls=%fused_computation | custom fusion | bytes 33792 | tf_op jit(solution)/shard_map/jit(_take)/gather | solution.py:58
  91.9 17.4 %fusion = f32[65536]{0:T(1024)} fusion(f32[32]{0:T(128)S(1)} %copy-done.2, bf16[256,65536]{1,0:T(8,128)(2,1)} %param.5, bf16[256,32]{1,0:T(8,128)(2,1)S(1)} %gather_fusion, pred[256]{0:T(512)(128)(4,1)S(1)} %get-tuple-element.2, pred[256]{0:T(512)(128)(4,1)S(1)} %get-tuple-element.8), kind=kOutput, calls=%fused_computation.2 | convolution fusion | flops 1079984128 | bytes 33833600 | tf_op jit(solution)/shard_map/bo,bc->oc/dot_general | solution.py:62
  109.4 36.0 %all-reduce.3.cloned.1.call-done = f32[8,64,128]{2,1,0:T(8,128)} async-done(((f32[8,64,128]{2,1,0:T(8,128)}), f32[8,64,128]{2,1,0:T(8,128)}) %all-reduce.3.cloned.1.call-update) | async-done | bytes 262160 | tf_op jit(solution)/shard_map/psum | solution.py:66
  146.2 1.9 %collective-permute-start.7 = (f32[1,64,128]{2,1,0:T(8,128)S(1)}, f32[1,64,128]{2,1,0:T(8,128)S(1)}, u32[]{:S(2)}, u32[]{:S(2)}) collective-permute-start(f32[1,64,128]{2,1,0:T(8,128)S(1)} %get-tuple-element.6), channel_id=1, source_target_pairs={{1,0},{2,1},{3,2},{4,3},{5,4},{6,5},{7,6},{9,8},{10,9},{11,10},{12... | collective-permute-start | bytes 98312 | tf_op jit(solution)/shard_map/ppermute | solution.py:20
  148.1 2.4 %collective-permute-start.8 = (f32[1,64,128]{2,1,0:T(8,128)S(1)}, f32[1,64,128]{2,1,0:T(8,128)S(1)}, u32[]{:S(2)}, u32[]{:S(2)}) collective-permute-start(f32[1,64,128]{2,1,0:T(8,128)S(1)} %get-tuple-element.7), channel_id=1, source_target_pairs={{0,1},{1,2},{2,3},{3,4},{4,5},{5,6},{6,7},{8,9},{9,10},{10,11},{11... | collective-permute-start | bytes 98312 | tf_op jit(solution)/shard_map/ppermute | solution.py:18
  150.5 1.5 constant_dynamic-slice_fusion
  152.0 2.2 %collective-permute-done.8 = f32[1,64,128]{2,1,0:T(8,128)S(1)} collective-permute-done((f32[1,64,128]{2,1,0:T(8,128)S(1)}, f32[1,64,128]{2,1,0:T(8,128)S(1)}, u32[]{:S(2)}, u32[]{:S(2)}) %collective-permute-start.8) | collective-permute-done | bytes 32800 | tf_op jit(solution)/shard_map/ppermute | solution.py:18
  154.2 1.2 select_maximum_fusion
  155.4 1.3 fusion.5
  (22 shorter events, 3.2 us)
Async XLA Ops:
  7.2 9.8 %copy-start = (s32[256,1]{0,1:T(1,128)S(1)}, s32[256,1]{0,1:T(1,128)}, u32[]{:S(2)}) copy-start(s32[256,1]{0,1:T(1,128)} %param.8) | copy-start | bytes 3076
  7.2 9.8 %copy-start.1 = (s32[256]{0:T(256)S(1)}, s32[256]{0:T(256)}, u32[]{:S(2)}) copy-start(s32[256]{0:T(256)} %param.9) | copy-start | bytes 3076
  7.2 138.2 %all-reduce.3.cloned.1.call-start = ((), (), s32[]{:S(2)}) async-start(), calls=%async_computation | async-start | bytes 524288 | tf_op jit(solution)/shard_map/psum | solution.py:66
  7.2 9.8 %collective-permute-start = (bf16[8192,32]{0,1:T(8,128)(2,1)}, bf16[8192,32]{0,1:T(8,128)(2,1)S(1)}, u32[]{:S(2)}, u32[]{:S(2)}) collective-permute-start(bf16[8192,32]{0,1:T(8,128)(2,1)} %param.6), channel_id=1, source_target_pairs={{0,1},{1,2},{2,3},{3,4},{4,5},{5,6},{6,7},{7,0},{8,9},{9,10},{10,1... | collective-permute-start | bytes 1572872 | tf_op jit(solution)/shard_map/ppermute | solution.py:51
  18.0 9.6 %collective-permute-start.1 = (bf16[8192,32]{0,1:T(8,128)(2,1)S(1)}, bf16[8192,32]{0,1:T(8,128)(2,1)S(1)}, u32[]{:S(2)}, u32[]{:S(2)}) collective-permute-start(bf16[8192,32]{0,1:T(8,128)(2,1)S(1)} %collective-permute-done), channel_id=1, source_target_pairs={{0,1},{1,2},{2,3},{3,4},{4,5},{5,6},{6,7},{7,0},{8,9},{9,10},{10,1... | collective-permute-start | bytes 1572872 | tf_op jit(solution)/shard_map/ppermute | solution.py:51
  28.6 9.6 %collective-permute-start.2 = (bf16[8192,32]{0,1:T(8,128)(2,1)S(1)}, bf16[8192,32]{0,1:T(8,128)(2,1)S(1)}, u32[]{:S(2)}, u32[]{:S(2)}) collective-permute-start(bf16[8192,32]{0,1:T(8,128)(2,1)S(1)} %collective-permute-done.1), channel_id=1, source_target_pairs={{0,1},{1,2},{2,3},{3,4},{4,5},{5,6},{6,7},{7,0},{8,9},{9,10},{10,1... | collective-permute-start | bytes 1572872 | tf_op jit(solution)/shard_map/ppermute | solution.py:51
  30.2 61.7 %copy-start.2 = (f32[32]{0:T(128)S(1)}, f32[32]{0:T(128)}, u32[]{:S(2)}) copy-start(f32[32]{0:T(128)} %param.7) | copy-start | bytes 388
  39.2 9.6 %collective-permute-start.3 = (bf16[8192,32]{0,1:T(8,128)(2,1)S(1)}, bf16[8192,32]{0,1:T(8,128)(2,1)S(1)}, u32[]{:S(2)}, u32[]{:S(2)}) collective-permute-start(bf16[8192,32]{0,1:T(8,128)(2,1)S(1)} %collective-permute-done.2), channel_id=1, source_target_pairs={{0,1},{1,2},{2,3},{3,4},{4,5},{5,6},{6,7},{7,0},{8,9},{9,10},{10,1... | collective-permute-start | bytes 1572872 | tf_op jit(solution)/shard_map/ppermute | solution.py:51
  49.8 9.6 %collective-permute-start.4 = (bf16[8192,32]{0,1:T(8,128)(2,1)S(1)}, bf16[8192,32]{0,1:T(8,128)(2,1)S(1)}, u32[]{:S(2)}, u32[]{:S(2)}) collective-permute-start(bf16[8192,32]{0,1:T(8,128)(2,1)S(1)} %collective-permute-done.3), channel_id=1, source_target_pairs={{0,1},{1,2},{2,3},{3,4},{4,5},{5,6},{6,7},{7,0},{8,9},{9,10},{10,1... | collective-permute-start | bytes 1572872 | tf_op jit(solution)/shard_map/ppermute | solution.py:51
  60.4 9.6 %collective-permute-start.5 = (bf16[8192,32]{0,1:T(8,128)(2,1)S(1)}, bf16[8192,32]{0,1:T(8,128)(2,1)S(1)}, u32[]{:S(2)}, u32[]{:S(2)}) collective-permute-start(bf16[8192,32]{0,1:T(8,128)(2,1)S(1)} %collective-permute-done.4), channel_id=1, source_target_pairs={{0,1},{1,2},{2,3},{3,4},{4,5},{5,6},{6,7},{7,0},{8,9},{9,10},{10,1... | collective-permute-start | bytes 1572872 | tf_op jit(solution)/shard_map/ppermute | solution.py:51
  71.0 9.7 %collective-permute-start.6 = (bf16[8192,32]{0,1:T(8,128)(2,1)S(1)}, bf16[8192,32]{0,1:T(8,128)(2,1)S(1)}, u32[]{:S(2)}, u32[]{:S(2)}) collective-permute-start(bf16[8192,32]{0,1:T(8,128)(2,1)S(1)} %collective-permute-done.5), channel_id=1, source_target_pairs={{0,1},{1,2},{2,3},{3,4},{4,5},{5,6},{6,7},{7,0},{8,9},{9,10},{10,1... | collective-permute-start | bytes 1572872 | tf_op jit(solution)/shard_map/ppermute | solution.py:51
  146.2 5.8 %collective-permute-start.7 = (f32[1,64,128]{2,1,0:T(8,128)S(1)}, f32[1,64,128]{2,1,0:T(8,128)S(1)}, u32[]{:S(2)}, u32[]{:S(2)}) collective-permute-start(f32[1,64,128]{2,1,0:T(8,128)S(1)} %get-tuple-element.6), channel_id=1, source_target_pairs={{1,0},{2,1},{3,2},{4,3},{5,4},{6,5},{7,6},{9,8},{10,9},{11,10},{12... | collective-permute-start | bytes 98312 | tf_op jit(solution)/shard_map/ppermute | solution.py:20
  148.1 6.1 %collective-permute-start.8 = (f32[1,64,128]{2,1,0:T(8,128)S(1)}, f32[1,64,128]{2,1,0:T(8,128)S(1)}, u32[]{:S(2)}, u32[]{:S(2)}) collective-permute-start(f32[1,64,128]{2,1,0:T(8,128)S(1)} %get-tuple-element.7), channel_id=1, source_target_pairs={{0,1},{1,2},{2,3},{3,4},{4,5},{5,6},{6,7},{8,9},{9,10},{10,11},{11... | collective-permute-start | bytes 98312 | tf_op jit(solution)/shard_map/ppermute | solution.py:18
Sparse Core Ops, SparseCore 0:
  109.5 35.8 all-reduce.2
